TPU v7x, 512 devices: a whole 4x4x16 slice. The times are simulated.
512 devices in a mesh: gx: 32 (over x, y, core), gy: 16 (over z).
Axes of the slice: x: 4, y: 4, z: 16, core: 2. Of those that a mesh axis runs over, the one named last changes fastest.
Arguments:
- schur_blocks: float32 [32, 16, 768, 768], P('gx', 'gy'), may hold values from -32 to 32, as said below
- basis: float32 [32, 16, 32, 768], P('gx', 'gy'), may hold values from -0.21875 to 0.21875
- loads: float32 [32, 16, 16, 768], P('gx', 'gy'), may hold values from -64 to 64
- coarse_inverse: float32 [16384, 16384], P(('gx', 'gy')), may hold values from -0.09375 to 0.09375
- iface_map: int32 [32, 16, 768], P('gx', 'gy'), may hold values from 0 to 767, as said below
- coarse_slot: int32 [512], replicated, may hold values from 0 to 511, each once
Outputs:
- solution: float32 [32, 16, 16, 768], P('gx', 'gy')
Inputs may be any that keep to these rules, and one draw needn't show every extreme that they name: `schur_blocks`: each block is symmetric. `iface_map`: for every subdomain the map is a permutation of 0 to 767 that maps each aligned block of 128 cells onto itself. `coarse_slot`: every subdomain has its own coarse block number.
All inputs are finite; a program needn't handle non-finite values.
Results may differ from a plain program's by a relative error of at most 0.0001.
Values sent between devices are 32-bit elements; how exact they have to be, the bound alone decides.
No kernel may reach another device: no remote copies, remote signals or barrier semaphores. Data moves between devices by JAX's collectives and lax.ppermute only.
A program may use at most 128 MiB of HBM per device.

v0:
```python
import jax
import jax.numpy as jnp
from jax import lax
from jax.sharding import PartitionSpec as P

EW = 256
ES = 128
ITERS = 3
highest = lax.Precision.HIGHEST
epsilon = 1e-06


def padded(block, sides, width):
    for axis, dim in sides:
        count = lax.axis_size(axis)
        forward = [(i, i + 1) for i in range(count - 1)]
        backward = [(target, source) for source, target in forward]
        low = lax.ppermute(
            lax.slice_in_dim(block, block.shape[dim] - width, None, axis=dim), axis, forward
        )
        high = lax.ppermute(lax.slice_in_dim(block, 0, width, axis=dim), axis, backward)
        block = jnp.concatenate([low, block, high], axis=dim)
    return block


def edge_stacks(layout):
    column_edges = jnp.stack([layout[:, :EW], layout[:, EW : 2 * EW]])
    row_edges = jnp.stack([layout[:, 2 * EW : 2 * EW + ES], layout[:, 2 * EW + ES :]])
    return (column_edges, row_edges)


def add_edges(values, position, across, along):
    outside = jnp.concatenate([across[0], across[3], along[0], along[3]], axis=1)
    return values + jnp.take(outside, position, axis=1)


def assemble(values, position, inverse):
    column_edges, row_edges = edge_stacks(jnp.take(values, inverse, axis=1))
    across = padded(column_edges, (("gy", 0),), 1)
    along = padded(row_edges, (("gx", 0),), 1)
    return add_edges(values, position, across, along)


def per_device(schur_blocks, basis, loads, coarse_inverse, iface_map, coarse_slot):
    schur_block = schur_blocks[0, 0]
    local_basis = basis[0, 0]
    position = iface_map[0, 0]
    inverse = jnp.argsort(position)
    mode_count = local_basis.shape[0]
    domain_count = coarse_slot.shape[0]
    reordered = jnp.take(
        coarse_inverse.reshape(mode_count, domain_count, mode_count), coarse_slot, axis=1
    )
    reordered = reordered.reshape(mode_count, domain_count * mode_count)
    residual = assemble(loads[0, 0], position, inverse)
    solution = jnp.zeros_like(residual)
    for iteration in range(ITERS):
        lifted = lax.dot_general(
            lax.all_gather(
                lax.dot_general(
                    residual,
                    local_basis,
                    (((1,), (1,)), ((), ())),
                    precision=highest,
                    preferred_element_type=jnp.float32,
                ),
                ("gx", "gy"),
                axis=1,
                tiled=True,
            ),
            reordered,
            (((1,), (1,)), ((), ())),
            precision=highest,
            preferred_element_type=jnp.float32,
        )
        spread = jnp.dot(lifted, local_basis, precision=highest, preferred_element_type=jnp.float32)
        column_edges, row_edges = edge_stacks(jnp.take(spread, inverse, axis=1))
        across = padded(column_edges, (("gy", 0),), 1)
        along = padded(row_edges, (("gx", 0),), 1)
        search = residual + add_edges(spread, position, across, along)
        local_image = jnp.dot(
            search, schur_block, precision=highest, preferred_element_type=jnp.float32
        )
        applied = assemble(local_image, position, inverse)
        totals = lax.psum(
            (jnp.sum(residual * applied, axis=1), jnp.sum(applied * applied, axis=1)), ("gx", "gy")
        )
        stride = (totals[0] / (totals[1] + epsilon))[:, None]
        solution = solution + stride * search
        residual = residual - stride * applied
    return solution[None, None]


def solution(mesh):
    placed = (
        P("gx", "gy", None, None),
        P("gx", "gy", None, None),
        P("gx", "gy", None, None),
        P(("gx", "gy"), None),
        P("gx", "gy", None),
        P(),
    )
    return jax.shard_map(
        per_device, mesh=mesh, in_specs=placed, out_specs=P("gx", "gy", None, None), check_vma=False
    )
```

profile of v0, /device:TPU:1, one launch (start us, length us, event | category | flops | bytes accessed | tf_op | source)
XLA Modules:
  0.0 1102.9 jit_solution(14531170180641245100)
XLA Ops:
  7.4 4.4 sort.17
  14.6 4.4 collective-permute-start
  20.3 4.0 collective-permute-start.2
  32.6 6.4 reshape.19
  39.0 11.5 %copy.97 = f32[32,512,32]{2,0,1:T(8,128)} copy(f32[32,512,32]{2,1,0:T(8,128)} %reshape.19) | data formatting | bytes 4194304 | tf_op jit(solution)/shard_map/reshape | solution.py:52
  50.5 7.7 gather_fusion
  58.3 11.5 %copy.98 = f32[32,512,32]{2,1,0:T(8,128)} copy(f32[32,512,32]{2,0,1:T(8,128)} %bitcast.179) | data formatting | bytes 4194304 | tf_op jit(solution)/shard_map/jit(_take)/gather | solution.py:51
  69.8 7.4 gather.10
  78.1 160.3 %all-gather.7.cloned.1.call-done = f32[512,32,16]{1,2,0:T(8,128)} async-done(((f32[1,32,16]{1,2,0:T(8,128)}), f32[512,32,16]{1,2,0:T(8,128)}) %all-gather.7.cloned.1.call-update) | async-done | bytes 1048592 | tf_op jit(solution)/shard_map/all_gather | solution.py:59
  238.4 5.5 copy.96
  263.7 3.6 collective-permute-done.7
  272.4 4.3 collective-permute-start.8
  287.6 106.4 %all-reduce.2 = (f32[16]{0:T(128)S(1)}, f32[16]{0:T(128)S(1)}) all-reduce(f32[16]{0:T(128)S(1)} %get-tuple-element.13, f32[16]{0:T(128)S(1)} %get-tuple-element.12), channel_id=1, replica_groups=mesh['gx'=32,'gy'=16] {'gx','gy'}, use_global_device_ids=true, to_apply=%region_2.4 | all-reduce | flops 32 | bytes 256 | tf_op jit(solution)/shard_map/psum | solution.py:85
  395.6 193.8 %all-gather.9.cloned.1.call-done = f32[512,32,16]{1,2,0:T(8,128)} async-done(((f32[1,32,16]{1,2,0:T(8,128)}), f32[512,32,16]{1,2,0:T(8,128)}) %all-gather.9.cloned.1.call-update) | async-done | bytes 1048592 | tf_op jit(solution)/shard_map/all_gather | solution.py:59
  589.5 5.6 copy.103
  595.0 3.7 reshape.158
  614.1 3.6 collective-permute-done.15
  622.7 4.3 collective-permute-start.16
  638.0 106.4 %all-reduce.1 = (f32[16]{0:T(128)S(1)}, f32[16]{0:T(128)S(1)}) all-reduce(f32[16]{0:T(128)S(1)} %get-tuple-element.11, f32[16]{0:T(128)S(1)} %get-tuple-element.10), channel_id=1, replica_groups=mesh['gx'=32,'gy'=16] {'gx','gy'}, use_global_device_ids=true, to_apply=%region_6.8 | all-reduce | flops 32 | bytes 256 | tf_op jit(solution)/shard_map/psum | solution.py:85
  745.3 193.9 %all-gather.11.cloned.1.call-done = f32[512,32,16]{1,2,0:T(8,128)} async-done(((f32[1,32,16]{1,2,0:T(8,128)}), f32[512,32,16]{1,2,0:T(8,128)}) %all-gather.11.cloned.1.call-update) | async-done | bytes 1048592 | tf_op jit(solution)/shard_map/all_gather | solution.py:59
  939.2 5.6 copy.108
  964.8 3.6 collective-permute-done.23
  973.5 4.3 collective-permute-start.24
  988.7 106.4 %all-reduce = (f32[16]{0:T(128)S(1)}, f32[16]{0:T(128)S(1)}) all-reduce(f32[16]{0:T(128)S(1)} %get-tuple-element.9, f32[16]{0:T(128)S(1)} %get-tuple-element.8), channel_id=1, replica_groups=mesh['gx'=32,'gy'=16] {'gx','gy'}, use_global_device_ids=true, to_apply=%region_10.12 | all-reduce | flops 32 | bytes 256 | tf_op jit(solution)/shard_map/psum | solution.py:85
  (212 shorter events, 119.5 us)
Async XLA Ops:
  6.5 231.9 %all-gather.7.cloned.1.call-start = ((), (), s32[]{:S(2)}) async-start(), calls=%async_computation | async-start | bytes 4202496 | tf_op jit(solution)/shard_map/all_gather | solution.py:59
  14.6 15.3 %collective-permute-start = (f32[1,16,256]{1,2,0:T(8,128)S(1)}, f32[1,16,256]{1,2,0:T(8,128)S(1)}, u32[]{:S(2)}, u32[]{:S(2)}) collective-permute-start(f32[1,16,256]{1,2,0:T(8,128)S(1)} %get-tuple-element.46), channel_id=1, source_target_pairs={{0,1},{1,2},{2,3},{3,4},{4,5},{5,6},{6,7},{7,8},{8,9},{9,10},{10,1... | collective-permute-start | bytes 49160 | tf_op jit(solution)/shard_map/ppermute | solution.py:18
  19.0 11.0 collective-permute-start.1
  20.3 7.1 collective-permute-start.2
  32.5 556.9 %all-gather.9.cloned.1.call-start = ((), (), s32[]{:S(2)}) async-start(), calls=%async_computation.1 | async-start | bytes 4202496 | tf_op jit(solution)/shard_map/all_gather | solution.py:59
  253.9 13.5 %collective-permute-start.4 = (f32[1,16,256]{1,2,0:T(8,128)S(1)}, f32[1,16,256]{1,2,0:T(8,128)S(1)}, u32[]{:S(2)}, u32[]{:S(2)}) collective-permute-start(f32[1,16,256]{1,2,0:T(8,128)S(1)} %get-tuple-element.42), channel_id=1, source_target_pairs={{0,1},{1,2},{2,3},{3,4},{4,5},{5,6},{6,7},{7,8},{8,9},{9,10},{10,1... | collective-permute-start | bytes 49160 | tf_op jit(solution)/shard_map/ppermute | solution.py:18
  257.0 10.3 collective-permute-start.5
  261.8 5.6 collective-permute-start.7
  272.4 13.4 %collective-permute-start.8 = (f32[1,16,256]{1,2,0:T(8,128)S(1)}, f32[1,16,256]{1,2,0:T(8,128)S(1)}, u32[]{:S(2)}, u32[]{:S(2)}) collective-permute-start(f32[1,16,256]{1,2,0:T(8,128)S(1)} %get-tuple-element.38), channel_id=1, source_target_pairs={{0,1},{1,2},{2,3},{3,4},{4,5},{5,6},{6,7},{7,8},{8,9},{9,10},{10,1... | collective-permute-start | bytes 49160 | tf_op jit(solution)/shard_map/ppermute | solution.py:18
  276.7 9.1 collective-permute-start.9
  280.2 5.6 collective-permute-start.11
  395.6 543.6 %all-gather.11.cloned.1.call-start = ((), (), s32[]{:S(2)}) async-start(), calls=%async_computation.2 | async-start | bytes 4202496 | tf_op jit(solution)/shard_map/all_gather | solution.py:59
  604.3 13.5 %collective-permute-start.12 = (f32[1,16,256]{1,2,0:T(8,128)S(1)}, f32[1,16,256]{1,2,0:T(8,128)S(1)}, u32[]{:S(2)}, u32[]{:S(2)}) collective-permute-start(f32[1,16,256]{1,2,0:T(8,128)S(1)} %get-tuple-element.34), channel_id=1, source_target_pairs={{0,1},{1,2},{2,3},{3,4},{4,5},{5,6},{6,7},{7,8},{8,9},{9,10},{10,1... | collective-permute-start | bytes 49160 | tf_op jit(solution)/shard_map/ppermute | solution.py:18
  607.3 10.5 collective-permute-start.13
  612.2 5.6 collective-permute-start.15
  622.7 13.4 %collective-permute-start.16 = (f32[1,16,256]{1,2,0:T(8,128)S(1)}, f32[1,16,256]{1,2,0:T(8,128)S(1)}, u32[]{:S(2)}, u32[]{:S(2)}) collective-permute-start(f32[1,16,256]{1,2,0:T(8,128)S(1)} %get-tuple-element.30), channel_id=1, source_target_pairs={{0,1},{1,2},{2,3},{3,4},{4,5},{5,6},{6,7},{7,8},{8,9},{9,10},{10,1... | collective-permute-start | bytes 49160 | tf_op jit(solution)/shard_map/ppermute | solution.py:18
  627.0 9.1 collective-permute-start.17
  630.5 5.6 collective-permute-start.19
  954.7 13.8 %collective-permute-start.20 = (f32[1,16,256]{1,2,0:T(8,128)S(1)}, f32[1,16,256]{1,2,0:T(8,128)S(1)}, u32[]{:S(2)}, u32[]{:S(2)}) collective-permute-start(f32[1,16,256]{1,2,0:T(8,128)S(1)} %get-tuple-element.26), channel_id=1, source_target_pairs={{0,1},{1,2},{2,3},{3,4},{4,5},{5,6},{6,7},{7,8},{8,9},{9,10},{10,1... | collective-permute-start | bytes 49160 | tf_op jit(solution)/shard_map/ppermute | solution.py:18
  957.8 10.7 collective-permute-start.21
  962.9 5.6 collective-permute-start.23
  973.5 13.3 %collective-permute-start.24 = (f32[1,16,256]{1,2,0:T(8,128)S(1)}, f32[1,16,256]{1,2,0:T(8,128)S(1)}, u32[]{:S(2)}, u32[]{:S(2)}) collective-permute-start(f32[1,16,256]{1,2,0:T(8,128)S(1)} %get-tuple-element.22), channel_id=1, source_target_pairs={{0,1},{1,2},{2,3},{3,4},{4,5},{5,6},{6,7},{7,8},{8,9},{9,10},{10,1... | collective-permute-start | bytes 49160 | tf_op jit(solution)/shard_map/ppermute | solution.py:18
  977.8 9.1 collective-permute-start.25
  981.2 5.6 collective-permute-start.27
  (38 other events, 1453.8 us)
Sparse Core Ops, SparseCore 0:
  32.7 205.7 all-gather.6
  395.7 193.6 all-gather.8
  745.5 193.7 all-gather.10
where the time goes:
time: 1110 us; the launch traced here: 1100 us
  waiting for transfers between devices  572 us (52%)
  blocking collectives  319 us (29%)
  local copies, waits for them, and re-layouts  99.1 us (9%)
  starting transfers between devices  72 us (6%)
  matrix products  16.6 us (1%)
  between operations  14.7 us (1%)
    all_gather x3, waiting for transfers between devices, per_device(): lax.all_gather(lax.dot_general(residual, local_basis, (((1,), (1,)), ((),...  548 us
    psum x3, blocking collectives, per_device(): lax.psum((jnp.sum(residual * applied, axis=1), jnp.sum(applied * applied,...  319 us
    ppermute x14, starting transfers between devices, padded(): lax.ppermute(lax.slice_in_dim(block, block.shape[dim] - width, None, axis...  47.4 us
    gather x3, local copies, waits for them, and re-layouts, per_device(): jnp.take(coarse_inverse.reshape(mode_count, domain_count, mode_count), co...  26.6 us
    ppermute x14, starting transfers between devices, padded(): lax.ppermute(lax.slice_in_dim(block, 0, width, axis=dim), axis, backward)  24.5 us
    ppermute x14, waiting for transfers between devices, padded(): lax.ppermute(lax.slice_in_dim(block, 0, width, axis=dim), axis, backward)  23.7 us
  transfers between devices with their start and end apart: 31, of which 10 were waited for; matrix products, arithmetic and copies ran while one was open for 4% of the time, Pallas kernels for 0%

commit v1 on v0

--- a/solution.py
+++ b/solution.py
@@ -83,7 +83,10 @@
         )
         applied = assemble(local_image, position, inverse)
         totals = lax.psum(
-            (jnp.sum(residual * applied, axis=1), jnp.sum(applied * applied, axis=1)), ("gx", "gy")
+            lax.psum(
+                (jnp.sum(residual * applied, axis=1), jnp.sum(applied * applied, axis=1)), "gx"
+            ),
+            "gy",
         )
         stride = (totals[0] / (totals[1] + epsilon))[:, None]
         solution = solution + stride * search

time: 1110 us -> 1070 us (0.964); the launches traced: 1100 us -> 1050 us
  blocking collectives: 319 us -> 252 us
  waiting for transfers between devices: 572 us -> 585 us
    psum x3, blocking collectives: 319 us -> 183 us  [per_device(): lax.psum((jnp.sum(residual * applied, axis=1), jnp.sum(applied * applied,...]
    psum x0 -> x3, blocking collectives: none -> 69.4 us  [per_device(): lax.psum(lax.psum((jnp.sum(residual * applied, axis=1), jnp.sum(applied *...]
    all_gather x3, waiting for transfers between devices: 548 us -> 561 us  [per_device(): lax.all_gather(lax.dot_general(residual, local_basis, (((1,), (1,)), ((),...]
where the time goes in v1:
time: 1070 us; the launch traced here: 1050 us
  waiting for transfers between devices  585 us (55%)
  blocking collectives  252 us (24%)
  local copies, waits for them, and re-layouts  99.4 us (9%)
  starting transfers between devices  71.8 us (7%)
  matrix products  16.6 us (2%)
  between operations  14.7 us (1%)
    all_gather x3, waiting for transfers between devices, per_device(): lax.all_gather(lax.dot_general(residual, local_basis, (((1,), (1,)), ((),...  561 us
    psum x3, blocking collectives, per_device(): lax.psum((jnp.sum(residual * applied, axis=1), jnp.sum(applied * applied,...  183 us
    psum x3, blocking collectives, per_device(): lax.psum(lax.psum((jnp.sum(residual * applied, axis=1), jnp.sum(applied *...  69.4 us
    ppermute x14, starting transfers between devices, padded(): lax.ppermute(lax.slice_in_dim(block, block.shape[dim] - width, None, axis...  47.4 us
    gather x3, local copies, waits for them, and re-layouts, per_device(): jnp.take(coarse_inverse.reshape(mode_count, domain_count, mode_count), co...  26.6 us
    ppermute x14, starting transfers between devices, padded(): lax.ppermute(lax.slice_in_dim(block, 0, width, axis=dim), axis, backward)  24.3 us
    ppermute x14, waiting for transfers between devices, padded(): lax.ppermute(lax.slice_in_dim(block, 0, width, axis=dim), axis, backward)  23.7 us
  transfers between devices with their start and end apart: 31, of which 10 were waited for; matrix products, arithmetic and copies ran while one was open for 4% of the time, Pallas kernels for 0%

profile of v1, /device:TPU:1, one launch (start us, length us, event | category | flops | bytes accessed | tf_op | source)
XLA Modules:
  0.0 1048.8 jit_solution(535824348541210417)
XLA Ops:
  7.4 4.4 sort.17
  14.6 4.4 collective-permute-start
  20.3 4.0 collective-permute-start.2
  32.6 6.4 reshape.19
  39.0 11.5 %copy.97 = f32[32,512,32]{2,0,1:T(8,128)} copy(f32[32,512,32]{2,1,0:T(8,128)} %reshape.19) | data formatting | bytes 4194304 | tf_op jit(solution)/shard_map/reshape | solution.py:52
  50.5 7.7 gather_fusion
  58.3 11.5 %copy.98 = f32[32,512,32]{2,1,0:T(8,128)} copy(f32[32,512,32]{2,0,1:T(8,128)} %bitcast.179) | data formatting | bytes 4194304 | tf_op jit(solution)/shard_map/jit(_take)/gather | solution.py:51
  69.8 7.4 gather.10
  78.0 160.4 %all-gather.7.cloned.1.call-done = f32[512,32,16]{1,2,0:T(8,128)} async-done(((f32[1,32,16]{1,2,0:T(8,128)}), f32[512,32,16]{1,2,0:T(8,128)}) %all-gather.7.cloned.1.call-update) | async-done | bytes 1048592 | tf_op jit(solution)/shard_map/all_gather | solution.py:59
  238.4 5.5 copy.96
  272.4 4.3 collective-permute-start.8
  287.6 61.0 %all-reduce.2 = (f32[16]{0:T(128)S(1)}, f32[16]{0:T(128)S(1)}) all-reduce(f32[16]{0:T(128)S(1)} %get-tuple-element.13, f32[16]{0:T(128)S(1)} %get-tuple-element.12), channel_id=1, replica_groups=mesh['gx'=32,'gy'=16] {'gx'}, use_global_device_ids=true, to_apply=%region_2.4 | all-reduce | flops 32 | bytes 256 | tf_op jit(solution)/shard_map/psum | solution.py:86
  348.6 23.1 %all-reduce.5 = (f32[16]{0:T(128)S(1)}, f32[16]{0:T(128)S(1)}) all-reduce(f32[16]{0:T(128)S(1)} %get-tuple-element.18, f32[16]{0:T(128)S(1)} %get-tuple-element.19), channel_id=1, replica_groups=mesh['gx'=32,'gy'=16] {'gy'}, use_global_device_ids=true, to_apply=%region_3.5 | all-reduce | flops 32 | bytes 256 | tf_op jit(solution)/shard_map/psum | solution.py:85
  373.3 200.3 %all-gather.9.cloned.1.call-done = f32[512,32,16]{1,2,0:T(8,128)} async-done(((f32[1,32,16]{1,2,0:T(8,128)}), f32[512,32,16]{1,2,0:T(8,128)}) %all-gather.9.cloned.1.call-update) | async-done | bytes 1048592 | tf_op jit(solution)/shard_map/all_gather | solution.py:59
  573.6 5.6 copy.103
  579.2 3.7 reshape.158
  606.9 4.3 collective-permute-start.16
  622.1 60.9 %all-reduce.1 = (f32[16]{0:T(128)S(1)}, f32[16]{0:T(128)S(1)}) all-reduce(f32[16]{0:T(128)S(1)} %get-tuple-element.11, f32[16]{0:T(128)S(1)} %get-tuple-element.10), channel_id=1, replica_groups=mesh['gx'=32,'gy'=16] {'gx'}, use_global_device_ids=true, to_apply=%region_8.10 | all-reduce | flops 32 | bytes 256 | tf_op jit(solution)/shard_map/psum | solution.py:86
  683.1 23.1 %all-reduce.4 = (f32[16]{0:T(128)S(1)}, f32[16]{0:T(128)S(1)}) all-reduce(f32[16]{0:T(128)S(1)} %get-tuple-element.16, f32[16]{0:T(128)S(1)} %get-tuple-element.17), channel_id=1, replica_groups=mesh['gx'=32,'gy'=16] {'gy'}, use_global_device_ids=true, to_apply=%region_9.11 | all-reduce | flops 32 | bytes 256 | tf_op jit(solution)/shard_map/psum | solution.py:85
  707.1 200.4 %all-gather.11.cloned.1.call-done = f32[512,32,16]{1,2,0:T(8,128)} async-done(((f32[1,32,16]{1,2,0:T(8,128)}), f32[512,32,16]{1,2,0:T(8,128)}) %all-gather.11.cloned.1.call-update) | async-done | bytes 1048592 | tf_op jit(solution)/shard_map/all_gather | solution.py:59
  907.5 5.6 copy.108
  941.8 4.3 collective-permute-start.24
  957.0 60.9 %all-reduce = (f32[16]{0:T(128)S(1)}, f32[16]{0:T(128)S(1)}) all-reduce(f32[16]{0:T(128)S(1)} %get-tuple-element.9, f32[16]{0:T(128)S(1)} %get-tuple-element.8), channel_id=1, replica_groups=mesh['gx'=32,'gy'=16] {'gx'}, use_global_device_ids=true, to_apply=%region_14.16 | all-reduce | flops 32 | bytes 256 | tf_op jit(solution)/shard_map/psum | solution.py:86
  1017.9 23.1 %all-reduce.3 = (f32[16]{0:T(128)S(1)}, f32[16]{0:T(128)S(1)}) all-reduce(f32[16]{0:T(128)S(1)} %get-tuple-element.14, f32[16]{0:T(128)S(1)} %get-tuple-element.15), channel_id=1, replica_groups=mesh['gx'=32,'gy'=16] {'gy'}, use_global_device_ids=true, to_apply=%region_15.17 | all-reduce | flops 32 | bytes 256 | tf_op jit(solution)/shard_map/psum | solution.py:85
  (215 shorter events, 130.3 us)
Async XLA Ops:
  6.5 231.9 %all-gather.7.cloned.1.call-start = ((), (), s32[]{:S(2)}) async-start(), calls=%async_computation | async-start | bytes 4202496 | tf_op jit(solution)/shard_map/all_gather | solution.py:59
  14.6 15.3 %collective-permute-start = (f32[1,16,256]{1,2,0:T(8,128)S(1)}, f32[1,16,256]{1,2,0:T(8,128)S(1)}, u32[]{:S(2)}, u32[]{:S(2)}) collective-permute-start(f32[1,16,256]{1,2,0:T(8,128)S(1)} %get-tuple-element.52), channel_id=1, source_target_pairs={{0,1},{1,2},{2,3},{3,4},{4,5},{5,6},{6,7},{7,8},{8,9},{9,10},{10,1... | collective-permute-start | bytes 49160 | tf_op jit(solution)/shard_map/ppermute | solution.py:18
  19.0 11.0 %collective-permute-start.1 = (f32[1,16,256]{1,2,0:T(8,128)S(1)}, f32[1,16,256]{1,2,0:T(8,128)S(1)}, u32[]{:S(2)}, u32[]{:S(2)}) collective-permute-start(f32[1,16,256]{1,2,0:T(8,128)S(1)} %get-tuple-element.53), channel_id=1, source_target_pairs={{1,0},{2,1},{3,2},{4,3},{5,4},{6,5},{7,6},{8,7},{9,8},{10,9},{11,1... | collective-permute-start | bytes 49160 | tf_op jit(solution)/shard_map/ppermute | solution.py:21
  20.3 7.1 collective-permute-start.2
  24.3 5.6 collective-permute-start.3
  32.5 541.1 %all-gather.9.cloned.1.call-start = ((), (), s32[]{:S(2)}) async-start(), calls=%async_computation.1 | async-start | bytes 4202496 | tf_op jit(solution)/shard_map/all_gather | solution.py:59
  253.8 13.5 %collective-permute-start.4 = (f32[1,16,256]{1,2,0:T(8,128)S(1)}, f32[1,16,256]{1,2,0:T(8,128)S(1)}, u32[]{:S(2)}, u32[]{:S(2)}) collective-permute-start(f32[1,16,256]{1,2,0:T(8,128)S(1)} %get-tuple-element.48), channel_id=1, source_target_pairs={{0,1},{1,2},{2,3},{3,4},{4,5},{5,6},{6,7},{7,8},{8,9},{9,10},{10,1... | collective-permute-start | bytes 49160 | tf_op jit(solution)/shard_map/ppermute | solution.py:18
  257.0 10.3 collective-permute-start.5
  261.8 5.6 collective-permute-start.7
  272.4 13.4 %collective-permute-start.8 = (f32[1,16,256]{1,2,0:T(8,128)S(1)}, f32[1,16,256]{1,2,0:T(8,128)S(1)}, u32[]{:S(2)}, u32[]{:S(2)}) collective-permute-start(f32[1,16,256]{1,2,0:T(8,128)S(1)} %get-tuple-element.44), channel_id=1, source_target_pairs={{0,1},{1,2},{2,3},{3,4},{4,5},{5,6},{6,7},{7,8},{8,9},{9,10},{10,1... | collective-permute-start | bytes 49160 | tf_op jit(solution)/shard_map/ppermute | solution.py:18
  276.7 9.1 collective-permute-start.9
  280.1 5.6 collective-permute-start.11
  373.2 534.3 %all-gather.11.cloned.1.call-start = ((), (), s32[]{:S(2)}) async-start(), calls=%async_computation.2 | async-start | bytes 4202496 | tf_op jit(solution)/shard_map/all_gather | solution.py:59
  588.4 13.5 %collective-permute-start.12 = (f32[1,16,256]{1,2,0:T(8,128)S(1)}, f32[1,16,256]{1,2,0:T(8,128)S(1)}, u32[]{:S(2)}, u32[]{:S(2)}) collective-permute-start(f32[1,16,256]{1,2,0:T(8,128)S(1)} %get-tuple-element.40), channel_id=1, source_target_pairs={{0,1},{1,2},{2,3},{3,4},{4,5},{5,6},{6,7},{7,8},{8,9},{9,10},{10,1... | collective-permute-start | bytes 49160 | tf_op jit(solution)/shard_map/ppermute | solution.py:18
  591.4 10.5 collective-permute-start.13
  596.3 5.6 collective-permute-start.15
  606.9 13.4 %collective-permute-start.16 = (f32[1,16,256]{1,2,0:T(8,128)S(1)}, f32[1,16,256]{1,2,0:T(8,128)S(1)}, u32[]{:S(2)}, u32[]{:S(2)}) collective-permute-start(f32[1,16,256]{1,2,0:T(8,128)S(1)} %get-tuple-element.36), channel_id=1, source_target_pairs={{0,1},{1,2},{2,3},{3,4},{4,5},{5,6},{6,7},{7,8},{8,9},{9,10},{10,1... | collective-permute-start | bytes 49160 | tf_op jit(solution)/shard_map/ppermute | solution.py:18
  611.2 9.1 collective-permute-start.17
  614.7 5.6 collective-permute-start.19
  923.0 13.5 %collective-permute-start.20 = (f32[1,16,256]{1,2,0:T(8,128)S(1)}, f32[1,16,256]{1,2,0:T(8,128)S(1)}, u32[]{:S(2)}, u32[]{:S(2)}) collective-permute-start(f32[1,16,256]{1,2,0:T(8,128)S(1)} %get-tuple-element.32), channel_id=1, source_target_pairs={{0,1},{1,2},{2,3},{3,4},{4,5},{5,6},{6,7},{7,8},{8,9},{9,10},{10,1... | collective-permute-start | bytes 49160 | tf_op jit(solution)/shard_map/ppermute | solution.py:18
  926.0 10.5 collective-permute-start.21
  941.8 13.3 %collective-permute-start.24 = (f32[1,16,256]{1,2,0:T(8,128)S(1)}, f32[1,16,256]{1,2,0:T(8,128)S(1)}, u32[]{:S(2)}, u32[]{:S(2)}) collective-permute-start(f32[1,16,256]{1,2,0:T(8,128)S(1)} %get-tuple-element.28), channel_id=1, source_target_pairs={{0,1},{1,2},{2,3},{3,4},{4,5},{5,6},{6,7},{7,8},{8,9},{9,10},{10,1... | collective-permute-start | bytes 49160 | tf_op jit(solution)/shard_map/ppermute | solution.py:18
  946.1 9.1 collective-permute-start.25
  949.5 5.6 collective-permute-start.27
  (38 other events, 1377.5 us)
Sparse Core Ops, SparseCore 0:
  32.7 205.7 all-gather.6
  373.3 200.2 all-gather.8
  707.3 200.2 all-gather.10
